TPU v7x, 128 devices: a whole 4x4x4 slice. The times are simulated.
128 devices in a mesh: lat: 8 (over z, core), lon: 16 (over y, x).
Axes of the slice: x: 4, y: 4, z: 4, core: 2. Of those that a mesh axis runs over, the one named last changes fastest.
Arguments:
- tokens: bfloat16 [128, 1024, 512], P('lat', 'lon'), may hold values from -6 to 6
- norm_gain: float32 [512], replicated, may hold values from 0.25 to 1.75
- w_query: bfloat16 [512, 512], replicated, may hold values from -1 to 1
- w_key: bfloat16 [512, 512], replicated, may hold values from -1 to 1
- w_value: bfloat16 [512, 512], replicated, may hold values from -0.25 to 0.25
- w_out: bfloat16 [512, 512], replicated, may hold values from -0.25 to 0.25
- pool_weight: bfloat16 [4, 64], replicated, may hold values from -0.75 to 0.75
- head_scale: float32 [8], replicated, may hold values from 0.5 to 32
- far_ids: int32 [16, 128, 48], P('lat', 'lon'), may hold values from 0 to 2047, as said below
- far_mask: int32 [16, 128, 48], P('lat', 'lon'), may hold values from 0 to 1, as said below
- mlp_gain: float32 [512], replicated, may hold values from 0.25 to 1.75
- w_up: bfloat16 [512, 2048], replicated, may hold values from -0.25 to 0.25
- w_down: bfloat16 [2048, 512], replicated, may hold values from -0.125 to 0.125
Outputs:
- result: bfloat16 [128, 1024, 512], P('lat', 'lon')
Inputs may be any that keep to these rules, and one draw needn't show every extreme that they name: `far_mask`: used slots come first in each block's list; every block uses at least 12 slots. `far_ids`: the tile of 16 x 64 tokens that one device holds is a grid of blocks; among all list slots of one such tile, used or not, the blocks of any one tile are named at most 6 times, and exactly 6 times for some tiles.
All inputs are finite; a program needn't handle non-finite values.
Results may differ from a plain program's by a relative error of at most 0.006.
The roundings to bfloat16 on the way count: a program that leaves them out, or rounds other values in their place, can miss the bound.
Values may be sent and summed in bfloat16 or wider, within the bound.
A program may use at most 128 MiB of HBM per device.

v0:
```python
import math
import jax
import jax.numpy as jnp
from jax import lax
from jax.sharding import PartitionSpec as P

BLK = 8
SUMROWS = 4
FAR = 48
eps = 1e-06


def padded_2(array, sides, width):
    for axis, dim in sides:
        size, length = (lax.axis_size(axis), array.shape[dim])
        up = [(i, (i + 1) % size) for i in range(size)]
        down = [(j, i) for i, j in up]
        last = lax.slice_in_dim(array, length - width, length, axis=dim)
        first = lax.slice_in_dim(array, 0, width, axis=dim)
        before = lax.ppermute(last, axis, up)
        after = lax.ppermute(first, axis, down)
        array = jnp.concatenate([before, array, after], axis=dim)
    return array


def rms_scale(values, scale_gain):
    wide = values.astype(jnp.float32)
    mean_square = jnp.mean(wide * wide, axis=-1, keepdims=True)
    return (wide * lax.rsqrt(mean_square + eps) * scale_gain).astype(jnp.bfloat16)


def project(values, weight):
    flat = values.reshape(-1, values.shape[-1])
    output = jnp.dot(flat, weight, preferred_element_type=jnp.float32).astype(jnp.bfloat16)
    return output.reshape(values.shape[:-1] + (weight.shape[1],))


def to_blocks(grid):
    row_count, col_count, feature = grid.shape
    shaped = grid.reshape(row_count // BLK, BLK, col_count // BLK, BLK, feature)
    return shaped.transpose(0, 2, 1, 3, 4).reshape(
        row_count // BLK, col_count // BLK, BLK * BLK, feature
    )


def local(
    tokens,
    norm_gain,
    w_query,
    w_key,
    w_value,
    w_out,
    pool_weight,
    head_scale,
    far_ids,
    far_mask,
    mlp_gain,
    w_up,
    w_down,
):
    tok_rows, tok_cols, feature = tokens.shape
    blk_rows = tok_rows // BLK
    blk_cols = tok_cols // BLK
    head_count = head_scale.shape[0]
    head_size = feature // head_count
    lat_count = lax.axis_size("lat")
    lon_count = lax.axis_size("lon")
    lat_index = lax.axis_index("lat")
    normed = rms_scale(tokens, norm_gain)
    query = project(normed, w_query)
    w_pair = jnp.concatenate([w_key, w_value], axis=1)
    paired = project(normed, w_pair)
    blocks = to_blocks(normed).reshape(blk_rows * blk_cols, BLK * BLK, feature)
    pooled = jnp.einsum("rt,btd->brd", pool_weight, blocks, preferred_element_type=jnp.float32)
    pooled = pooled.astype(jnp.bfloat16).reshape(blk_rows * blk_cols * SUMROWS, feature)
    padded = padded_2(paired, (("lat", 0), ("lon", 1)), BLK)
    global_cols = blk_cols * lon_count
    global_row = far_ids // global_cols
    global_col = far_ids % global_cols
    owner = global_row // blk_rows * lon_count + global_col // blk_cols
    inner_block = global_row % blk_rows * blk_cols + global_col % blk_cols
    gathered_index = owner * (blk_rows * blk_cols) + inner_block
    listed = gathered_index.reshape(-1)
    sub_rows = jnp.arange(SUMROWS, dtype=jnp.int32)
    listed_rows = (listed[:, None] * SUMROWS + sub_rows[None, :]).reshape(-1)
    summary = project(pooled, w_pair)
    every_pair = lax.all_gather(summary, ("lat", "lon"), axis=0, tiled=True)
    far_pair = jnp.take(every_pair, listed_rows, axis=0)
    far_pair = far_pair.reshape(blk_rows, blk_cols, FAR * SUMROWS, 2 * feature)
    place = jnp.arange(tok_rows + 2 * BLK, dtype=jnp.int32) + lat_index * tok_rows - BLK
    row_valid = (place >= 0) & (place < tok_rows * lat_count)
    query_blocks = to_blocks(query)
    score_scale = head_scale * (1.0 / math.sqrt(head_size))
    near_width = 3 * BLK * BLK

    def one_row(row_index):
        strip = lax.dynamic_slice_in_dim(padded, row_index * BLK, 3 * BLK, 0)
        shaped = strip.reshape(3 * BLK, blk_cols + 2, BLK, 2, head_count, head_size)
        key_grid = shaped[:, :, :, 0]
        value_grid = shaped[:, :, :, 1]
        row_query = lax.dynamic_index_in_dim(query_blocks, row_index, 0, keepdims=False)
        query_heads = row_query.reshape(blk_cols, BLK * BLK, head_count, head_size)
        far_rows = lax.dynamic_index_in_dim(far_pair, row_index, 0, keepdims=False)
        far_heads = far_rows.reshape(blk_cols, FAR * SUMROWS, 2, head_count, head_size)
        scores = []
        for offset in range(3):
            part_score = jnp.einsum(
                "cqhd,rckhd->chqrk",
                query_heads,
                key_grid[:, offset : offset + blk_cols],
                preferred_element_type=jnp.float32,
            )
            scores.append(part_score.reshape(blk_cols, head_count, BLK * BLK, near_width))
        scores.append(
            jnp.einsum(
                "cqhd,ckhd->chqk",
                query_heads,
                far_heads[:, :, 0],
                preferred_element_type=jnp.float32,
            )
        )
        score = jnp.concatenate(scores, axis=-1) * score_scale[None, :, None, None]
        strip_valid = lax.dynamic_slice_in_dim(row_valid, row_index * BLK, 3 * BLK, 0)
        near_valid = jnp.broadcast_to(strip_valid[:, None], (3 * BLK, BLK)).reshape(-1)
        row_mask = lax.dynamic_index_in_dim(far_mask, row_index, 0, keepdims=False)
        far_valid = jnp.repeat(row_mask > 0, SUMROWS, axis=1)
        near_all = jnp.concatenate([near_valid, near_valid, near_valid])
        valid = jnp.concatenate(
            [jnp.broadcast_to(near_all[None, :], (blk_cols, near_all.shape[0])), far_valid], axis=1
        )
        keep = valid[:, None, None, :]
        highest = jnp.max(jnp.where(keep, score, -1e30), axis=-1, keepdims=True)
        expo = jnp.exp(jnp.where(keep, score - highest, -1e30))
        weights = (expo / jnp.sum(expo, axis=-1, keepdims=True)).astype(jnp.bfloat16)
        mixed = jnp.einsum(
            "chqk,ckhd->cqhd",
            weights[..., 3 * near_width :],
            far_heads[:, :, 1],
            preferred_element_type=jnp.float32,
        )
        for offset in range(3):
            part_weight = weights[..., offset * near_width : (offset + 1) * near_width].reshape(
                blk_cols, head_count, BLK * BLK, 3 * BLK, BLK
            )
            mixed = mixed + jnp.einsum(
                "chqrk,rckhd->cqhd",
                part_weight,
                value_grid[:, offset : offset + blk_cols],
                preferred_element_type=jnp.float32,
            )
        return mixed.astype(jnp.bfloat16).reshape(blk_cols, BLK * BLK, feature)

    attended = lax.map(one_row, jnp.arange(blk_rows, dtype=jnp.int32))
    attn = (
        attended.reshape(blk_rows, blk_cols, BLK, BLK, feature)
        .transpose(0, 2, 1, 3, 4)
        .reshape(tok_rows * tok_cols, feature)
    )
    mixed = (
        tokens.reshape(-1, feature).astype(jnp.float32)
        + jnp.dot(attn, w_out, preferred_element_type=jnp.float32)
    ).astype(jnp.bfloat16)
    normed_two = rms_scale(mixed, mlp_gain)
    hidden = jax.nn.gelu(
        jnp.dot(normed_two, w_up, preferred_element_type=jnp.float32), approximate=True
    ).astype(jnp.bfloat16)
    result = (
        mixed.astype(jnp.float32) + jnp.dot(hidden, w_down, preferred_element_type=jnp.float32)
    ).astype(jnp.bfloat16)
    return result.reshape(tok_rows, tok_cols, feature)


def solution(mesh):
    return jax.shard_map(
        local,
        mesh=mesh,
        in_specs=(
            P("lat", "lon", None),
            P(),
            P(),
            P(),
            P(),
            P(),
            P(),
            P(),
            P("lat", "lon", None),
            P("lat", "lon", None),
            P(),
            P(),
            P(),
        ),
        out_specs=P("lat", "lon", None),
        check_vma=False,
    )
```

profile of v0, /device:TPU:1, one launch (start us, length us, event | category | flops | bytes accessed | tf_op | source)
XLA Modules:
  0.0 528.9 jit_solution(14609142763297510466)
XLA Ops:
  31.4 6.1 %collective-permute-done = bf16[8,64,1024]{2,1,0:T(8,128)(2,1)S(1)} collective-permute-done((bf16[8,64,1024]{2,1,0:T(8,128)(2,1)}, bf16[8,64,1024]{2,1,0:T(8,128)(2,1)S(1)}, u32[]{:S(2)}, u32[]{:S(2)}) %collective-permute-start) | collective-permute-done | bytes 1048608 | tf_op jit(solution)/shard_map/ppermute | solution.py:20
  42.7 3.8 collective-permute-start.3
  46.6 13.8 %collective-permute-done.2 = bf16[32,8,1024]{2,1,0:T(8,128)(2,1)S(1)} collective-permute-done((bf16[32,8,1024]{2,1,0:T(8,128)(2,1)S(1)}, bf16[32,8,1024]{2,1,0:T(8,128)(2,1)S(1)}, u32[]{:S(2)}, u32[]{:S(2)}) %collective-permute-start.2) | collective-permute-done | bytes 524320 | tf_op jit(solution)/shard_map/ppermute | solution.py:20
  60.4 5.4 %pad_maximum_fusion = bf16[32,80,1024]{2,1,0:T(8,128)(2,1)} fusion(bf16[32,8,1024]{2,1,0:T(8,128)(2,1)S(1)} %collective-permute-done.3, bf16[8,64,1024]{2,1,0:T(8,128)(2,1)} %collective-permute-done.1, bf16[16,64,1024]{2,1,0:T(8,128)(2,1)S(1)} %bitcast.161, bf16[8,64,1024]{2,1,0:T(8,128)(2,1)S(1)} %collective-permute-done, ...), kind=kLoop, calls=%fused_computation.59 | loop fusion | flops 26214400 | bytes 10485760 | tf_op jit(solution)/shard_map/concatenate | solution.py:22
  65.8 38.2 %all-gather.2.cloned.1.call-done = bf16[8192,1024]{1,0:T(8,128)(2,1)} async-done(((bf16[64,1024]{1,0:T(8,128)(2,1)}), bf16[8192,1024]{1,0:T(8,128)(2,1)}) %all-gather.2.cloned.1.call-update) | async-done | bytes 16777232 | tf_op jit(solution)/shard_map/all_gather | solution.py:87
  104.0 23.9 %gather_fusion = bf16[3072,1024]{1,0:T(8,128)(2,1)} fusion(bf16[8192,1024]{1,0:T(8,128)(2,1)} %all-gather.2.cloned.1.call-done, s32[3072]{0:T(1024)S(1)} %broadcast_clamp_fusion), kind=kCustom, calls=%fused_computation | custom fusion | bytes 12595200 | tf_op jit(solution)/shard_map/jit(_take)/gather | solution.py:88
  128.0 11.1 %copy.73 = bf16[2,8,192,1024]{2,3,1,0:T(8,128)(2,1)} copy(bf16[2,8,192,1024]{3,2,1,0:T(8,128)(2,1)} %bitcast.159) | data formatting | bytes 12582912 | tf_op jit(solution)/shard_map/jit(_take)/gather | solution.py:88
  139.0 7.6 %broadcast_select_fusion = bf16[2,8,192,1024]{2,3,1,0:T(8,128)(2,1)} fusion(bf16[2,8,192,1024]{2,3,1,0:T(8,128)(2,1)} %copy.73, pred[2,8,192]{2,1,0:T(8,128)(4,1)S(1)} %compare_and_fusion), kind=kLoop, calls=%fused_computation.58 | loop fusion | flops 3145728 | bytes 12585984 | tf_op jit(solution)/shard_map/jit(_take)/select_n | solution.py:88
  146.6 364.2 %while.10 = (s32[]{:T(128)}, bf16[2,8,64,512]{3,2,1,0:T(8,128)(2,1)}, s32[2]{0:T(128)S(1)}, bf16[2,8,192,1024]{2,3,1,0:T(8,128)(2,1)}, pred[32]{0:T(512)(128)(4,...) while((s32[]{:T(128)}, ...), condition=%wide.region_4.5_spmd, body=%wide.region_1.4_spmd.sunk | while | flops 850403584 | bytes 223804016 | solution.py:153
  147.7 4.6 constant_dynamic-slice_fusion.11
  152.4 11.2 %reshape.180 = bf16[24,10,8,2,8,64]{5,4,3,2,1,0:T(8,128)(2,1)} reshape(bf16[24,80,1024]{2,1,0:T(8,128)(2,1)} %constant_dynamic-slice_fusion.11) | data formatting | bytes 7864320 | tf_op jit(solution)/shard_map/while/body/eval_jaxpr/reshape | solution.py:98
  163.6 5.6 %fusion.127 = (bf16[24,10,8,1,8,64]{5,4,3,2,1,0:T(8,128)(2,1)}, bf16[24,10,8,1,8,64]{5,4,3,2,1,0:T(8,128)(2,1)S(1)}) fusion(bf16[24,10,8,2,8,64]{5,4,3,2,1,0:T(8,128)(2,1)} %reshape.180), kind=kLoop, calls=%fused_computation.135.clone.1 | loop fusion | bytes 7864320 | tf_op jit(solution)/shard_map/while/body/eval_jaxpr/slice | solution.py:100
  169.2 4.9 copy.160
  183.0 4.0 copy.161
  187.0 6.8 %copy.162 = f32[8,8,64,192]{3,2,1,0:T(8,128)} copy(f32[8,8,64,192]{2,3,1,0:T(8,128)} %bitcast.150) | data formatting | bytes 6291456 | tf_op jit(solution)/shard_map/while/body/eval_jaxpr/reshape | solution.py:113
  197.5 4.1 copy.163
  201.6 6.3 %copy.164 = f32[8,8,64,192]{3,2,1,0:T(8,128)} copy(f32[8,8,64,192]{2,3,1,0:T(8,128)} %bitcast.151) | data formatting | bytes 6291456 | tf_op jit(solution)/shard_map/while/body/eval_jaxpr/reshape | solution.py:113
  211.6 3.9 copy.165
  215.5 6.3 %copy.166 = f32[8,8,64,192]{3,2,1,0:T(8,128)} copy(f32[8,8,64,192]{2,3,1,0:T(8,128)} %bitcast.152) | data formatting | bytes 6291456 | tf_op jit(solution)/shard_map/while/body/eval_jaxpr/reshape | solution.py:113
  227.0 41.4 %fusion.131 = (f32[8,8,64]{2,1,0:T(8,128)S(1)}, f32[8,8,64,768]{3,2,1,0:T(8,128)}) fusion(pred[8,768]{1,0:T(8,128)(4,1)S(1)} %pad_add_fusion.5, f32[8]{0:T(128)S(1)} %get-tuple-element.209, f32[8,8,64,192]{3,2,1,0:T(8,128)S(1)} %fusion.126, f32[8,8,64,192]{3,2,1,0:T(8,128)} %copy.162, f32[8,8,64,192]{3,2,1,0:T(8,128)} %copy.164, ...), kind=kOutput, calls=%fused_computation.137.clone.1 | output fusion | flops 37749504 | bytes 25188384 | tf_op jit(solution)/shard_map/while/body/eval_jaxpr/sub | solution.py:133
  268.4 8.0 %divide_convert_fusion.2 = bf16[8,8,64,768]{3,2,1,0:T(8,128)(2,1)} fusion(f32[8,8,64,768]{3,2,1,0:T(8,128)} %get-tuple-element.165, f32[8,8,64]{2,1,0:T(8,128)S(1)} %get-tuple-element.166), kind=kLoop, calls=%fused_computation.3.clone.1 | loop fusion | flops 6291456 | bytes 18890752 | tf_op jit(solution)/shard_map/while/body/eval_jaxpr/convert_element_type | solution.py:134
  276.5 7.2 %fusion.132 = (bf16[8,8,64,192]{3,2,1,0:T(8,128)(2,1)}, bf16[8,8,64,192]{3,2,1,0:T(8,128)(2,1)}, bf16[8,8,64,192]{3,2,1,0:T(8,128)(2,1)}) fusion(bf16[8,8,64,768]{3,2,1,0:T(8,128)(2,1)} %divide_convert_fusion.2), kind=kLoop, calls=%fused_computation.136.clone.1 | loop fusion | bytes 9437184 | tf_op jit(solution)/shard_map/while/body/eval_jaxpr/slice | solution.py:142
  283.7 4.5 copy.169
  288.1 8.2 %fusion.135 = f32[8,8,64,64,1]{3,2,4,1,0:T(8,128)} fusion(bf16[8,8,64,24,8]{2,4,3,1,0:T(8,128)(2,1)} %bitcast.156, bf16[24,10,8,1,8,64]{5,4,3,2,1,0:T(8,128)(2,1)} %get-tuple-element.168), kind=kOutput, calls=%fused_computation.24.clone.1 | convolution fusion | flops 100663296 | bytes 4587520 | tf_op jit(solution)/shard_map/while/body/eval_jaxpr/chqrk,rckhd->cqhd/dot_general | solution.py:145
  296.3 4.7 copy.168
  301.0 8.2 %fusion.134 = f32[8,8,64,64,1]{3,2,4,1,0:T(8,128)} fusion(bf16[8,8,64,24,8]{2,4,3,1,0:T(8,128)(2,1)} %bitcast.158, bf16[24,10,8,1,8,64]{5,4,3,2,1,0:T(8,128)(2,1)} %get-tuple-element.168), kind=kOutput, calls=%fused_computation.22.clone.1 | convolution fusion | flops 100663296 | bytes 4587520 | tf_op jit(solution)/shard_map/while/body/eval_jaxpr/chqrk,rckhd->cqhd/dot_general | solution.py:145
  309.2 4.5 copy.167
  313.7 7.0 %fusion.133 = f32[8,8,64,64,1]{3,2,4,1,0:T(8,128)S(1)} fusion(bf16[8,8,64,24,8]{2,4,3,1,0:T(8,128)(2,1)} %bitcast.157, bf16[24,10,8,1,8,64]{5,4,3,2,1,0:T(8,128)(2,1)} %get-tuple-element.168), kind=kOutput, calls=%fused_computation.20.clone.1 | convolution fusion | flops 100663296 | bytes 4587520 | tf_op jit(solution)/shard_map/while/body/eval_jaxpr/chqrk,rckhd->cqhd/dot_general | solution.py:145
  328.0 4.6 constant_dynamic-slice_fusion.11
  332.6 11.2 %reshape.180 = bf16[24,10,8,2,8,64]{5,4,3,2,1,0:T(8,128)(2,1)} reshape(bf16[24,80,1024]{2,1,0:T(8,128)(2,1)} %constant_dynamic-slice_fusion.11) | data formatting | bytes 7864320 | tf_op jit(solution)/shard_map/while/body/eval_jaxpr/reshape | solution.py:98
  343.8 5.6 %fusion.127 = (bf16[24,10,8,1,8,64]{5,4,3,2,1,0:T(8,128)(2,1)}, bf16[24,10,8,1,8,64]{5,4,3,2,1,0:T(8,128)(2,1)S(1)}) fusion(bf16[24,10,8,2,8,64]{5,4,3,2,1,0:T(8,128)(2,1)} %reshape.180), kind=kLoop, calls=%fused_computation.135.clone.1 | loop fusion | bytes 7864320 | tf_op jit(solution)/shard_map/while/body/eval_jaxpr/slice | solution.py:100
  349.5 4.9 copy.160
  363.3 4.0 copy.161
  367.3 6.5 %copy.162 = f32[8,8,64,192]{3,2,1,0:T(8,128)} copy(f32[8,8,64,192]{2,3,1,0:T(8,128)} %bitcast.150) | data formatting | bytes 6291456 | tf_op jit(solution)/shard_map/while/body/eval_jaxpr/reshape | solution.py:113
  377.4 4.1 copy.163
  381.5 6.3 %copy.164 = f32[8,8,64,192]{3,2,1,0:T(8,128)} copy(f32[8,8,64,192]{2,3,1,0:T(8,128)} %bitcast.151) | data formatting | bytes 6291456 | tf_op jit(solution)/shard_map/while/body/eval_jaxpr/reshape | solution.py:113
  391.5 3.9 copy.165
  395.5 6.3 %copy.166 = f32[8,8,64,192]{3,2,1,0:T(8,128)} copy(f32[8,8,64,192]{2,3,1,0:T(8,128)} %bitcast.152) | data formatting | bytes 6291456 | tf_op jit(solution)/shard_map/while/body/eval_jaxpr/reshape | solution.py:113
  407.0 41.5 %fusion.131 = (f32[8,8,64]{2,1,0:T(8,128)S(1)}, f32[8,8,64,768]{3,2,1,0:T(8,128)}) fusion(pred[8,768]{1,0:T(8,128)(4,1)S(1)} %pad_add_fusion.5, f32[8]{0:T(128)S(1)} %get-tuple-element.209, f32[8,8,64,192]{3,2,1,0:T(8,128)S(1)} %fusion.126, f32[8,8,64,192]{3,2,1,0:T(8,128)} %copy.162, f32[8,8,64,192]{3,2,1,0:T(8,128)} %copy.164, ...), kind=kOutput, calls=%fused_computation.137.clone.1 | output fusion | flops 37749504 | bytes 25188384 | tf_op jit(solution)/shard_map/while/body/eval_jaxpr/sub | solution.py:133
  448.4 8.0 %divide_convert_fusion.2 = bf16[8,8,64,768]{3,2,1,0:T(8,128)(2,1)} fusion(f32[8,8,64,768]{3,2,1,0:T(8,128)} %get-tuple-element.165, f32[8,8,64]{2,1,0:T(8,128)S(1)} %get-tuple-element.166), kind=kLoop, calls=%fused_computation.3.clone.1 | loop fusion | flops 6291456 | bytes 18890752 | tf_op jit(solution)/shard_map/while/body/eval_jaxpr/convert_element_type | solution.py:134
  456.5 7.2 %fusion.132 = (bf16[8,8,64,192]{3,2,1,0:T(8,128)(2,1)}, bf16[8,8,64,192]{3,2,1,0:T(8,128)(2,1)}, bf16[8,8,64,192]{3,2,1,0:T(8,128)(2,1)}) fusion(bf16[8,8,64,768]{3,2,1,0:T(8,128)(2,1)} %divide_convert_fusion.2), kind=kLoop, calls=%fused_computation.136.clone.1 | loop fusion | bytes 9437184 | tf_op jit(solution)/shard_map/while/body/eval_jaxpr/slice | solution.py:142
  463.6 4.5 copy.169
  468.1 8.2 %fusion.135 = f32[8,8,64,64,1]{3,2,4,1,0:T(8,128)} fusion(bf16[8,8,64,24,8]{2,4,3,1,0:T(8,128)(2,1)} %bitcast.156, bf16[24,10,8,1,8,64]{5,4,3,2,1,0:T(8,128)(2,1)} %get-tuple-element.168), kind=kOutput, calls=%fused_computation.24.clone.1 | convolution fusion | flops 100663296 | bytes 4587520 | tf_op jit(solution)/shard_map/while/body/eval_jaxpr/chqrk,rckhd->cqhd/dot_general | solution.py:145
  476.3 4.9 copy.168
  481.2 8.2 %fusion.134 = f32[8,8,64,64,1]{3,2,4,1,0:T(8,128)} fusion(bf16[8,8,64,24,8]{2,4,3,1,0:T(8,128)(2,1)} %bitcast.158, bf16[24,10,8,1,8,64]{5,4,3,2,1,0:T(8,128)(2,1)} %get-tuple-element.168), kind=kOutput, calls=%fused_computation.22.clone.1 | convolution fusion | flops 100663296 | bytes 4587520 | tf_op jit(solution)/shard_map/while/body/eval_jaxpr/chqrk,rckhd->cqhd/dot_general | solution.py:145
  489.4 4.5 copy.167
  493.9 7.0 %fusion.133 = f32[8,8,64,64,1]{3,2,4,1,0:T(8,128)S(1)} fusion(bf16[8,8,64,24,8]{2,4,3,1,0:T(8,128)(2,1)} %bitcast.157, bf16[24,10,8,1,8,64]{5,4,3,2,1,0:T(8,128)(2,1)} %get-tuple-element.168), kind=kOutput, calls=%fused_computation.20.clone.1 | convolution fusion | flops 100663296 | bytes 4587520 | tf_op jit(solution)/shard_map/while/body/eval_jaxpr/chqrk,rckhd->cqhd/dot_general | solution.py:145
  514.4 7.4 %fusion.43 = bf16[1024,512]{1,0:T(8,128)(2,1)} fusion(bf16[1024,512]{1,0:T(8,128)(2,1)S(1)} %get-tuple-element.101, bf16[2048,512]{1,0:T(8,128)(2,1)S(1)} %copy-done, bf16[512,2048]{1,0:T(8,128)(2,1)} %param.26, f32[512]{0:T(512)S(1)} %copy-done.13, f32[1024]{0:T(1024)S(1)} %add_rsqrt_fusion.1), kind=kOutput, calls=%fused_computation.67 | convolution fusion | flops 4317511680 | bytes 6297600 | tf_op jit(solution)/shard_map/dot_general | solution.py:168
  (122 shorter events, 85.6 us)
Async XLA Ops:
  6.5 507.8 %copy-start = (bf16[2048,512]{1,0:T(8,128)(2,1)S(1)}, bf16[2048,512]{1,0:T(8,128)(2,1)}, u32[]{:S(2)}) copy-start(bf16[2048,512]{1,0:T(8,128)(2,1)} %param.27) | copy-start | bytes 6291460
  6.5 5.2 copy-start.12
  6.5 97.5 %all-gather.2.cloned.1.call-start = ((), (), s32[]{:S(2)}) async-start(), calls=%async_computation | async-start | bytes 16908288 | tf_op jit(solution)/shard_map/all_gather | solution.py:87
  11.6 7.0 %copy-start.7 = (bf16[16,64,512]{2,1,0:T(8,128)(2,1)}, bf16[16,64,512]{2,1,0:T(8,128)(2,1)S(1)}, u32[]{:S(2)}) copy-start(bf16[16,64,512]{2,1,0:T(8,128)(2,1)S(1)} %multiply_convert_fusion) | copy-start | bytes 3145732
  18.6 1.3 copy-start.5
  19.9 4.6 copy-start.11
  21.5 16.0 %collective-permute-start = (bf16[8,64,1024]{2,1,0:T(8,128)(2,1)}, bf16[8,64,1024]{2,1,0:T(8,128)(2,1)S(1)}, u32[]{:S(2)}, u32[]{:S(2)}) collective-permute-start(bf16[8,64,1024]{2,1,0:T(8,128)(2,1)} %bitcast.38), channel_id=1, source_target_pairs={{0,16},{16,32},{32,48},{48,64},{64,80},{80,96},{96,112},{112,0},{1... | collective-permute-start | bytes 3145736 | tf_op jit(solution)/shard_map/ppermute | solution.py:20
  24.5 15.8 %collective-permute-start.1 = (bf16[8,64,1024]{2,1,0:T(8,128)(2,1)}, bf16[8,64,1024]{2,1,0:T(8,128)(2,1)}, u32[]{:S(2)}, u32[]{:S(2)}) collective-permute-start(bf16[8,64,1024]{2,1,0:T(8,128)(2,1)} %bitcast.40), channel_id=1, source_target_pairs={{16,0},{32,16},{48,32},{64,48},{80,64},{96,80},{112,96},{0,112},{1... | collective-permute-start | bytes 3145736 | tf_op jit(solution)/shard_map/ppermute | solution.py:21
  28.1 3.2 copy-start.14
  28.1 3.2 copy-start.10
  30.2 16.3 %copy-start.8 = (s32[2,8,192]{2,1,0:T(8,128)S(1)}, s32[2,8,192]{2,1,0:T(8,128)}, u32[]{:S(2)}) copy-start(s32[2,8,192]{2,1,0:T(8,128)} %copy.71) | copy-start | bytes 36868
  31.3 29.1 %copy-start.6 = (bf16[1024,1024]{1,0:T(8,128)(2,1)S(1)}, bf16[1024,1024]{1,0:T(8,128)(2,1)}, u32[]{:S(2)}) copy-start(bf16[1024,1024]{1,0:T(8,128)(2,1)} %copy-done.5) | copy-start | bytes 6291460
  41.5 18.9 %collective-permute-start.2 = (bf16[32,8,1024]{2,1,0:T(8,128)(2,1)S(1)}, bf16[32,8,1024]{2,1,0:T(8,128)(2,1)S(1)}, u32[]{:S(2)}, u32[]{:S(2)}) collective-permute-start(bf16[32,8,1024]{2,1,0:T(8,128)(2,1)S(1)} %get-tuple-element.96), channel_id=1, source_target_pairs={{0,1},{1,2},{2,3},{3,4},{4,5},{5,6},{6,7},{7,8},{8,9},{9,10},{10,1... | collective-permute-start | bytes 1572872 | tf_op jit(solution)/shard_map/ppermute | solution.py:20
  42.7 17.6 %collective-permute-start.3 = (bf16[32,8,1024]{2,1,0:T(8,128)(2,1)S(1)}, bf16[32,8,1024]{2,1,0:T(8,128)(2,1)S(1)}, u32[]{:S(2)}, u32[]{:S(2)}) collective-permute-start(bf16[32,8,1024]{2,1,0:T(8,128)(2,1)S(1)} %get-tuple-element.97), channel_id=1, source_target_pairs={{1,0},{2,1},{3,2},{4,3},{5,4},{6,5},{7,6},{8,7},{9,8},{10,9},{11,1... | collective-permute-start | bytes 1572872 | tf_op jit(solution)/shard_map/ppermute | solution.py:21
  139.0 7.6 %copy-start.9 = (s32[2,8,48]{2,1,0:T(8,128)S(1)}, s32[2,8,48]{2,1,0:T(8,128)}, u32[]{:S(2)}) copy-start(s32[2,8,48]{2,1,0:T(8,128)} %param.24) | copy-start | bytes 9220
  225.0 2.0 copy-start.1
  313.7 7.0 %copy-start.2 = (bf16[1,8,192,1024]{2,3,1,0:T(8,128)(2,1)S(1)}, bf16[1,8,192,1024]{2,3,1,0:T(8,128)(2,1)}, u32[]{:S(2)}) copy-start(bf16[1,8,192,1024]{2,3,1,0:T(8,128)(2,1)} %copy-done.1) | copy-start | bytes 9437188 | tf_op jit(solution)/shard_map/while
  313.7 7.0 %copy-start.3 = (f32[8,8,64,64,1]{3,2,4,1,0:T(8,128)S(1)}, f32[8,8,64,64,1]{3,2,4,1,0:T(8,128)}, u32[]{:S(2)}) copy-start(f32[8,8,64,64,1]{3,2,4,1,0:T(8,128)} %fusion.135) | copy-start | bytes 3145732 | tf_op jit(solution)/shard_map/while
  313.7 7.0 %copy-start.4 = (f32[8,8,64,64,1]{3,2,4,1,0:T(8,128)S(1)}, f32[8,8,64,64,1]{3,2,4,1,0:T(8,128)}, u32[]{:S(2)}) copy-start(f32[8,8,64,64,1]{3,2,4,1,0:T(8,128)} %fusion.134) | copy-start | bytes 3145732 | tf_op jit(solution)/shard_map/while
  404.9 2.0 copy-start.1
  493.9 7.0 %copy-start.2 = (bf16[1,8,192,1024]{2,3,1,0:T(8,128)(2,1)S(1)}, bf16[1,8,192,1024]{2,3,1,0:T(8,128)(2,1)}, u32[]{:S(2)}) copy-start(bf16[1,8,192,1024]{2,3,1,0:T(8,128)(2,1)} %copy-done.1) | copy-start | bytes 9437188 | tf_op jit(solution)/shard_map/while
  493.9 7.0 %copy-start.3 = (f32[8,8,64,64,1]{3,2,4,1,0:T(8,128)S(1)}, f32[8,8,64,64,1]{3,2,4,1,0:T(8,128)}, u32[]{:S(2)}) copy-start(f32[8,8,64,64,1]{3,2,4,1,0:T(8,128)} %fusion.135) | copy-start | bytes 3145732 | tf_op jit(solution)/shard_map/while
  493.9 7.0 %copy-start.4 = (f32[8,8,64,64,1]{3,2,4,1,0:T(8,128)S(1)}, f32[8,8,64,64,1]{3,2,4,1,0:T(8,128)}, u32[]{:S(2)}) copy-start(f32[8,8,64,64,1]{3,2,4,1,0:T(8,128)} %fusion.134) | copy-start | bytes 3145732 | tf_op jit(solution)/shard_map/while
  510.8 3.6 copy-start.13
Sparse Core Ops, SparseCore 0:
  16.2 87.7 all-gather.1
where the time goes:
time: 539 us; the launch traced here: 529 us
  local copies, waits for them, and re-layouts  227 us (42%)
  other arithmetic  117 us (22%)
  matrix products  92.3 us (17%)
  waiting for transfers between devices  60.9 us (11%)
  between operations  13.8 us (3%)
  loops' own time  9.32 us (2%)
  starting transfers between devices  8.05 us (1%)
    sub x2, other arithmetic, one_row(): expo = jnp.exp(jnp.where(keep, score - highest, -1e+30))  82.9 us
    dot_general x6, matrix products, one_row(): jnp.einsum('chqrk,rckhd->cqhd', part_weight, value_grid[:, offset:offset...  46.7 us
    slice x8, local copies, waits for them, and re-layouts, one_row(): weights[..., offset * near_width:(offset + 1) * near_width]  41.8 us
    reshape x6, local copies, waits for them, and re-layouts, one_row(): part_score.reshape(blk_cols, head_count, BLK * BLK, near_width)  38.6 us
    all_gather x1, waiting for transfers between devices, local(): every_pair = lax.all_gather(summary, ('lat', 'lon'), axis=0, tiled=True)  38.2 us
    gather x2, local copies, waits for them, and re-layouts, local(): far_pair = jnp.take(every_pair, listed_rows, axis=0)  35 us
    dot_general x6, local copies, waits for them, and re-layouts, one_row(): jnp.einsum('cqhd,rckhd->chqrk', query_heads, key_grid[:, offset:offset +...  24 us
    reshape x2, local copies, waits for them, and re-layouts, one_row(): shaped = strip.reshape(3 * BLK, blk_cols + 2, BLK, 2, head_count, head_size)  22.4 us
  transfers between devices with their start and end apart: 5, of which 4 were waited for; matrix products, arithmetic and copies ran while one was open for 3% of the time, Pallas kernels for 0%

commit v1 on v0

--- a/solution.py
+++ b/solution.py
@@ -84,7 +84,10 @@
     sub_rows = jnp.arange(SUMROWS, dtype=jnp.int32)
     listed_rows = (listed[:, None] * SUMROWS + sub_rows[None, :]).reshape(-1)
     summary = project(pooled, w_pair)
-    every_pair = lax.all_gather(summary, ("lat", "lon"), axis=0, tiled=True)
+    every_pair = jnp.concatenate(
+        lax.all_to_all(jnp.stack([summary] * lax.axis_size(("lat", "lon"))), ("lat", "lon"), 0, 0),
+        axis=0,
+    )
     far_pair = jnp.take(every_pair, listed_rows, axis=0)
     far_pair = far_pair.reshape(blk_rows, blk_cols, FAR * SUMROWS, 2 * feature)
     place = jnp.arange(tok_rows + 2 * BLK, dtype=jnp.int32) + lat_index * tok_rows - BLK

time: 539 us -> 723 us (1.34)
  the two profiles are of different devices: /device:TPU:1 before, /device:TPU:12 now
where the time goes in v1:
time: 723 us; the launch traced here: 713 us
  local copies, waits for them, and re-layouts  234 us (32%)
  waiting for transfers between devices  234 us (32%)
  other arithmetic  117 us (16%)
  matrix products  91.7 us (13%)
  starting transfers between devices  25.7 us (4%)
  loops' own time  10.3 us (1%)
    ppermute x2, waiting for transfers between devices, padded_2(): before = lax.ppermute(last, axis, up)  201 us
    sub x2, other arithmetic, one_row(): expo = jnp.exp(jnp.where(keep, score - highest, -1e+30))  82.9 us
    dot_general x6, matrix products, one_row(): jnp.einsum('chqrk,rckhd->cqhd', part_weight, value_grid[:, offset:offset...  46.8 us
    slice x8, local copies, waits for them, and re-layouts, one_row(): weights[..., offset * near_width:(offset + 1) * near_width]  42.2 us
    reshape x6, local copies, waits for them, and re-layouts, one_row(): part_score.reshape(blk_cols, head_count, BLK * BLK, near_width)  38.6 us
    gather x2, local copies, waits for them, and re-layouts, local(): far_pair = jnp.take(every_pair, listed_rows, axis=0)  34.9 us
    ppermute x2, waiting for transfers between devices, padded_2(): after = lax.ppermute(first, axis, down)  32.5 us
    dot_general x6, local copies, waits for them, and re-layouts, one_row(): jnp.einsum('cqhd,rckhd->chqrk', query_heads, key_grid[:, offset:offset +...  23.9 us
  transfers between devices with their start and end apart: 5, of which 3 were waited for; matrix products, arithmetic and copies ran while one was open for 2% of the time, Pallas kernels for 0%

profile of v1, /device:TPU:12, one launch (start us, length us, event | category | flops | bytes accessed | tf_op | source)
XLA Modules:
  0.0 713.0 jit_solution(5621016355881696295)
XLA Ops:
  8.9 6.2 stack.2
  15.1 10.8 %all-to-all-start = ((bf16[128,64,1024]{2,1,0:T(8,128)(2,1)}), bf16[128,64,1024]{2,1,0:T(8,128)(2,1)}, u32[]{:S(2)}, u32[]{:S(2)}) async-start(bf16[128,64,1024]{2,1,0:T(8,128)(2,1)} %stack.2), calls=%async_computation | async-start | bytes 33554432 | tf_op jit(solution)/shard_map/all_to_all | solution.py:88
  41.4 117.5 %collective-permute-done = bf16[8,64,1024]{2,1,0:T(8,128)(2,1)S(1)} collective-permute-done((bf16[8,64,1024]{2,1,0:T(8,128)(2,1)}, bf16[8,64,1024]{2,1,0:T(8,128)(2,1)S(1)}, u32[]{:S(2)}, u32[]{:S(2)}) %collective-permute-start) | collective-permute-done | bytes 1048608 | tf_op jit(solution)/shard_map/ppermute | solution.py:20
  160.1 11.6 %collective-permute-start.2 = (bf16[32,8,1024]{2,1,0:T(8,128)(2,1)S(1)}, bf16[32,8,1024]{2,1,0:T(8,128)(2,1)S(1)}, u32[]{:S(2)}, u32[]{:S(2)}) collective-permute-start(bf16[32,8,1024]{2,1,0:T(8,128)(2,1)S(1)} %get-tuple-element.96), channel_id=1, source_target_pairs={{0,1},{1,2},{2,3},{3,4},{4,5},{5,6},{6,7},{7,8},{8,9},{9,10},{10,1... | collective-permute-start | bytes 1572872 | tf_op jit(solution)/shard_map/ppermute | solution.py:20
  171.8 83.8 %collective-permute-done.2 = bf16[32,8,1024]{2,1,0:T(8,128)(2,1)S(1)} collective-permute-done((bf16[32,8,1024]{2,1,0:T(8,128)(2,1)S(1)}, bf16[32,8,1024]{2,1,0:T(8,128)(2,1)S(1)}, u32[]{:S(2)}, u32[]{:S(2)}) %collective-permute-start.2) | collective-permute-done | bytes 524320 | tf_op jit(solution)/shard_map/ppermute | solution.py:20
  255.6 32.5 %collective-permute-done.3 = bf16[32,8,1024]{2,1,0:T(8,128)(2,1)S(1)} collective-permute-done((bf16[32,8,1024]{2,1,0:T(8,128)(2,1)S(1)}, bf16[32,8,1024]{2,1,0:T(8,128)(2,1)S(1)}, u32[]{:S(2)}, u32[]{:S(2)}) %collective-permute-start.3) | collective-permute-done | bytes 524320 | tf_op jit(solution)/shard_map/ppermute | solution.py:21
  288.1 5.4 pad_maximum_fusion
  293.5 23.9 %gather_fusion = bf16[3072,1024]{1,0:T(8,128)(2,1)} fusion(bf16[8192,1024]{1,0:T(8,128)(2,1)} %bitcast.32, s32[3072]{0:T(1024)S(1)} %broadcast_clamp_fusion), kind=kCustom, calls=%fused_computation | custom fusion | bytes 12595200 | tf_op jit(solution)/shard_map/jit(_take)/gather | solution.py:91
  317.4 11.0 %copy.73 = bf16[2,8,192,1024]{2,3,1,0:T(8,128)(2,1)} copy(bf16[2,8,192,1024]{3,2,1,0:T(8,128)(2,1)} %bitcast.160) | data formatting | bytes 12582912 | tf_op jit(solution)/shard_map/jit(_take)/gather | solution.py:91
  328.4 7.5 %broadcast_select_fusion = bf16[2,8,192,1024]{2,3,1,0:T(8,128)(2,1)} fusion(bf16[2,8,192,1024]{2,3,1,0:T(8,128)(2,1)} %copy.73, pred[2,8,192]{2,1,0:T(8,128)(4,1)S(1)} %compare_and_fusion), kind=kLoop, calls=%fused_computation.58 | loop fusion | flops 3145728 | bytes 12585984 | tf_op jit(solution)/shard_map/jit(_take)/select_n | solution.py:91
  336.0 365.8 %while.10 = (s32[]{:T(128)}, bf16[2,8,64,512]{3,2,1,0:T(8,128)(2,1)}, s32[2]{0:T(128)S(1)}, bf16[2,8,192,1024]{2,3,1,0:T(8,128)(2,1)}, pred[32]{0:T(512)(128)(4,...) while((s32[]{:T(128)}, ...), condition=%wide.region_4.5_spmd, body=%wide.region_1.4_spmd.sunk | while | flops 850403584 | bytes 223804016 | solution.py:156
  337.3 4.6 constant_dynamic-slice_fusion.11
  342.0 11.2 %reshape.186 = bf16[24,10,8,2,8,64]{5,4,3,2,1,0:T(8,128)(2,1)} reshape(bf16[24,80,1024]{2,1,0:T(8,128)(2,1)} %constant_dynamic-slice_fusion.11) | data formatting | bytes 7864320 | tf_op jit(solution)/shard_map/while/body/eval_jaxpr/reshape | solution.py:101
  353.2 5.6 fusion.127
  358.8 4.9 copy.160
  373.0 4.0 copy.161
  377.0 6.8 copy.162
  387.5 4.1 copy.163
  391.5 6.3 copy.164
  405.5 6.4 copy.166
  417.0 41.5 %fusion.131 = (f32[8,8,64]{2,1,0:T(8,128)S(1)}, f32[8,8,64,768]{3,2,1,0:T(8,128)}) fusion(pred[8,768]{1,0:T(8,128)(4,1)S(1)} %pad_add_fusion.5, f32[8]{0:T(128)S(1)} %get-tuple-element.209, f32[8,8,64,192]{3,2,1,0:T(8,128)S(1)} %fusion.126, f32[8,8,64,192]{3,2,1,0:T(8,128)} %copy.162, f32[8,8,64,192]{3,2,1,0:T(8,128)} %copy.164, ...), kind=kOutput, calls=%fused_computation.137.clone.1 | output fusion | flops 37749504 | bytes 25188384 | tf_op jit(solution)/shard_map/while/body/eval_jaxpr/sub | solution.py:136
  458.4 8.0 %divide_convert_fusion.2 = bf16[8,8,64,768]{3,2,1,0:T(8,128)(2,1)} fusion(f32[8,8,64,768]{3,2,1,0:T(8,128)} %get-tuple-element.165, f32[8,8,64]{2,1,0:T(8,128)S(1)} %get-tuple-element.166), kind=kLoop, calls=%fused_computation.3.clone.1 | loop fusion | flops 6291456 | bytes 18890752 | tf_op jit(solution)/shard_map/while/body/eval_jaxpr/convert_element_type | solution.py:137
  466.5 7.3 %fusion.132 = (bf16[8,8,64,192]{3,2,1,0:T(8,128)(2,1)}, bf16[8,8,64,192]{3,2,1,0:T(8,128)(2,1)}, bf16[8,8,64,192]{3,2,1,0:T(8,128)(2,1)}) fusion(bf16[8,8,64,768]{3,2,1,0:T(8,128)(2,1)} %divide_convert_fusion.2), kind=kLoop, calls=%fused_computation.136.clone.1 | loop fusion | bytes 9437184 | tf_op jit(solution)/shard_map/while/body/eval_jaxpr/slice | solution.py:145
  473.8 4.5 copy.169
  478.3 8.2 %fusion.135 = f32[8,8,64,64,1]{3,2,4,1,0:T(8,128)} fusion(bf16[8,8,64,24,8]{2,4,3,1,0:T(8,128)(2,1)} %bitcast.157, bf16[24,10,8,1,8,64]{5,4,3,2,1,0:T(8,128)(2,1)} %get-tuple-element.168), kind=kOutput, calls=%fused_computation.24.clone.1 | convolution fusion | flops 100663296 | bytes 4587520 | tf_op jit(solution)/shard_map/while/body/eval_jaxpr/chqrk,rckhd->cqhd/dot_general | solution.py:148
  486.5 4.7 copy.168
  491.2 8.2 %fusion.134 = f32[8,8,64,64,1]{3,2,4,1,0:T(8,128)} fusion(bf16[8,8,64,24,8]{2,4,3,1,0:T(8,128)(2,1)} %bitcast.159, bf16[24,10,8,1,8,64]{5,4,3,2,1,0:T(8,128)(2,1)} %get-tuple-element.168), kind=kOutput, calls=%fused_computation.22.clone.1 | convolution fusion | flops 100663296 | bytes 4587520 | tf_op jit(solution)/shard_map/while/body/eval_jaxpr/chqrk,rckhd->cqhd/dot_general | solution.py:148
  499.4 4.5 copy.167
  503.9 7.0 fusion.133
  518.4 4.6 constant_dynamic-slice_fusion.11
  523.0 11.2 %reshape.186 = bf16[24,10,8,2,8,64]{5,4,3,2,1,0:T(8,128)(2,1)} reshape(bf16[24,80,1024]{2,1,0:T(8,128)(2,1)} %constant_dynamic-slice_fusion.11) | data formatting | bytes 7864320 | tf_op jit(solution)/shard_map/while/body/eval_jaxpr/reshape | solution.py:101
  534.3 5.6 fusion.127
  539.9 4.9 copy.160
  554.1 4.0 copy.161
  558.1 6.5 copy.162
  568.2 4.1 copy.163
  572.3 6.3 copy.164
  586.2 6.4 copy.166
  597.7 41.5 %fusion.131 = (f32[8,8,64]{2,1,0:T(8,128)S(1)}, f32[8,8,64,768]{3,2,1,0:T(8,128)}) fusion(pred[8,768]{1,0:T(8,128)(4,1)S(1)} %pad_add_fusion.5, f32[8]{0:T(128)S(1)} %get-tuple-element.209, f32[8,8,64,192]{3,2,1,0:T(8,128)S(1)} %fusion.126, f32[8,8,64,192]{3,2,1,0:T(8,128)} %copy.162, f32[8,8,64,192]{3,2,1,0:T(8,128)} %copy.164, ...), kind=kOutput, calls=%fused_computation.137.clone.1 | output fusion | flops 37749504 | bytes 25188384 | tf_op jit(solution)/shard_map/while/body/eval_jaxpr/sub | solution.py:136
  639.2 8.0 %divide_convert_fusion.2 = bf16[8,8,64,768]{3,2,1,0:T(8,128)(2,1)} fusion(f32[8,8,64,768]{3,2,1,0:T(8,128)} %get-tuple-element.165, f32[8,8,64]{2,1,0:T(8,128)S(1)} %get-tuple-element.166), kind=kLoop, calls=%fused_computation.3.clone.1 | loop fusion | flops 6291456 | bytes 18890752 | tf_op jit(solution)/shard_map/while/body/eval_jaxpr/convert_element_type | solution.py:137
  647.3 7.3 %fusion.132 = (bf16[8,8,64,192]{3,2,1,0:T(8,128)(2,1)}, bf16[8,8,64,192]{3,2,1,0:T(8,128)(2,1)}, bf16[8,8,64,192]{3,2,1,0:T(8,128)(2,1)}) fusion(bf16[8,8,64,768]{3,2,1,0:T(8,128)(2,1)} %divide_convert_fusion.2), kind=kLoop, calls=%fused_computation.136.clone.1 | loop fusion | bytes 9437184 | tf_op jit(solution)/shard_map/while/body/eval_jaxpr/slice | solution.py:145
  654.6 4.5 copy.169
  659.1 8.2 %fusion.135 = f32[8,8,64,64,1]{3,2,4,1,0:T(8,128)} fusion(bf16[8,8,64,24,8]{2,4,3,1,0:T(8,128)(2,1)} %bitcast.157, bf16[24,10,8,1,8,64]{5,4,3,2,1,0:T(8,128)(2,1)} %get-tuple-element.168), kind=kOutput, calls=%fused_computation.24.clone.1 | convolution fusion | flops 100663296 | bytes 4587520 | tf_op jit(solution)/shard_map/while/body/eval_jaxpr/chqrk,rckhd->cqhd/dot_general | solution.py:148
  667.3 4.9 copy.168
  672.2 8.2 %fusion.134 = f32[8,8,64,64,1]{3,2,4,1,0:T(8,128)} fusion(bf16[8,8,64,24,8]{2,4,3,1,0:T(8,128)(2,1)} %bitcast.159, bf16[24,10,8,1,8,64]{5,4,3,2,1,0:T(8,128)(2,1)} %get-tuple-element.168), kind=kOutput, calls=%fused_computation.22.clone.1 | convolution fusion | flops 100663296 | bytes 4587520 | tf_op jit(solution)/shard_map/while/body/eval_jaxpr/chqrk,rckhd->cqhd/dot_general | solution.py:148
  680.4 4.5 copy.167
  684.9 7.0 fusion.133
  705.3 7.4 %fusion.43 = bf16[1024,512]{1,0:T(8,128)(2,1)} fusion(bf16[1024,512]{1,0:T(8,128)(2,1)S(1)} %get-tuple-element.101, bf16[2048,512]{1,0:T(8,128)(2,1)S(1)} %copy-done, bf16[512,2048]{1,0:T(8,128)(2,1)} %param.26, f32[512]{0:T(512)S(1)} %copy-done.13, f32[1024]{0:T(1024)S(1)} %add_rsqrt_fusion.1), kind=kOutput, calls=%fused_computation.67 | convolution fusion | flops 4317511680 | bytes 6297600 | tf_op jit(solution)/shard_map/dot_general | solution.py:171
  (122 shorter events, 89.1 us)
Async XLA Ops:
  0.0 705.3 %copy-start = (bf16[2048,512]{1,0:T(8,128)(2,1)S(1)}, bf16[2048,512]{1,0:T(8,128)(2,1)}, u32[]{:S(2)}) copy-start(bf16[2048,512]{1,0:T(8,128)(2,1)} %param.27) | copy-start | bytes 6291460
  0.0 5.2 copy-start.12
  5.1 20.9 %copy-start.7 = (bf16[16,64,512]{2,1,0:T(8,128)(2,1)}, bf16[16,64,512]{2,1,0:T(8,128)(2,1)S(1)}, u32[]{:S(2)}) copy-start(bf16[16,64,512]{2,1,0:T(8,128)(2,1)S(1)} %multiply_convert_fusion) | copy-start | bytes 3145732
  15.1 278.4 %all-to-all-start = ((bf16[128,64,1024]{2,1,0:T(8,128)(2,1)}), bf16[128,64,1024]{2,1,0:T(8,128)(2,1)}, u32[]{:S(2)}, u32[]{:S(2)}) async-start(bf16[128,64,1024]{2,1,0:T(8,128)(2,1)} %stack.2), calls=%async_computation | async-start | bytes 33554432 | tf_op jit(solution)/shard_map/all_to_all | solution.py:88
  28.5 1.3 copy-start.5
  29.8 4.7 copy-start.11
  31.3 127.5 %collective-permute-start = (bf16[8,64,1024]{2,1,0:T(8,128)(2,1)}, bf16[8,64,1024]{2,1,0:T(8,128)(2,1)S(1)}, u32[]{:S(2)}, u32[]{:S(2)}) collective-permute-start(bf16[8,64,1024]{2,1,0:T(8,128)(2,1)} %bitcast.39), channel_id=1, source_target_pairs={{0,16},{16,32},{32,48},{48,64},{64,80},{80,96},{96,112},{112,0},{1... | collective-permute-start | bytes 3145736 | tf_op jit(solution)/shard_map/ppermute | solution.py:20
  31.5 127.4 %collective-permute-start.1 = (bf16[8,64,1024]{2,1,0:T(8,128)(2,1)}, bf16[8,64,1024]{2,1,0:T(8,128)(2,1)}, u32[]{:S(2)}, u32[]{:S(2)}) collective-permute-start(bf16[8,64,1024]{2,1,0:T(8,128)(2,1)} %bitcast.41), channel_id=1, source_target_pairs={{16,0},{32,16},{48,32},{64,48},{80,64},{96,80},{112,96},{0,112},{1... | collective-permute-start | bytes 3145736 | tf_op jit(solution)/shard_map/ppermute | solution.py:21
  38.1 3.2 copy-start.14
  38.1 3.2 copy-start.10
  40.2 131.5 %copy-start.8 = (s32[2,8,192]{2,1,0:T(8,128)S(1)}, s32[2,8,192]{2,1,0:T(8,128)}, u32[]{:S(2)}) copy-start(s32[2,8,192]{2,1,0:T(8,128)} %copy.71) | copy-start | bytes 36868
  41.3 246.8 %copy-start.6 = (bf16[1024,1024]{1,0:T(8,128)(2,1)S(1)}, bf16[1024,1024]{1,0:T(8,128)(2,1)}, u32[]{:S(2)}) copy-start(bf16[1024,1024]{1,0:T(8,128)(2,1)} %copy-done.5) | copy-start | bytes 6291460
  160.1 95.5 %collective-permute-start.2 = (bf16[32,8,1024]{2,1,0:T(8,128)(2,1)S(1)}, bf16[32,8,1024]{2,1,0:T(8,128)(2,1)S(1)}, u32[]{:S(2)}, u32[]{:S(2)}) collective-permute-start(bf16[32,8,1024]{2,1,0:T(8,128)(2,1)S(1)} %get-tuple-element.96), channel_id=1, source_target_pairs={{0,1},{1,2},{2,3},{3,4},{4,5},{5,6},{6,7},{7,8},{8,9},{9,10},{10,1... | collective-permute-start | bytes 1572872 | tf_op jit(solution)/shard_map/ppermute | solution.py:20
  171.7 116.4 %collective-permute-start.3 = (bf16[32,8,1024]{2,1,0:T(8,128)(2,1)S(1)}, bf16[32,8,1024]{2,1,0:T(8,128)(2,1)S(1)}, u32[]{:S(2)}, u32[]{:S(2)}) collective-permute-start(bf16[32,8,1024]{2,1,0:T(8,128)(2,1)S(1)} %get-tuple-element.97), channel_id=1, source_target_pairs={{1,0},{2,1},{3,2},{4,3},{5,4},{6,5},{7,6},{8,7},{9,8},{10,9},{11,1... | collective-permute-start | bytes 1572872 | tf_op jit(solution)/shard_map/ppermute | solution.py:21
  328.4 7.6 %copy-start.9 = (s32[2,8,48]{2,1,0:T(8,128)S(1)}, s32[2,8,48]{2,1,0:T(8,128)}, u32[]{:S(2)}) copy-start(s32[2,8,48]{2,1,0:T(8,128)} %param.24) | copy-start | bytes 9220
  415.0 2.0 copy-start.1
  503.9 7.0 copy-start.2
  503.9 7.0 copy-start.3
  503.9 7.0 copy-start.4
  595.7 2.0 copy-start.1
  684.9 7.0 copy-start.2
  684.9 7.0 copy-start.3
  684.9 7.0 copy-start.4
  701.7 3.6 copy-start.13
